TPU v7x, 32 devices: a whole 2x2x4 slice. The times are simulated.
32 devices in a mesh: rep: 4 (over z), shard: 8 (over y, x, core).
Axes of the slice: x: 2, y: 2, z: 4, core: 2. Of those that a mesh axis runs over, the one named last changes fastest.
Arguments:
- hidden_in: bfloat16 [8192, 2048], P(('rep', 'shard')), may hold values from -6 to 6
- cotangent: bfloat16 [8192, 2048], P(('rep', 'shard')), may hold values from -6 to 6
- lengths: int32 [32, 4], P(('rep', 'shard')), may hold values from 0 to 256, as said below
- offsets: int32 [32, 4], P(('rep', 'shard')), may hold values from 0 to 256, as said below
- projection_weight: bfloat16 [2048, 4096], P('shard'), may hold values from -0.125 to 0.125
- merge_weight: bfloat16 [2048, 2048], P('shard'), may hold values from -1 to 1
- expand_weight: bfloat16 [2048, 12288], P('shard'), may hold values from -0.125 to 0.125
- down_weight: bfloat16 [6144, 2048], P('shard'), may hold values from -0.078125 to 0.078125
- first_gain: bfloat16 [2048], P('shard'), may hold values from 0.099609375 to 1.8984375
- second_gain: bfloat16 [2048], P('shard'), may hold values from 0.099609375 to 1.8984375
- query_norm_scale: bfloat16 [128], P('shard'), may hold values from 0.099609375 to 1.8984375
- key_gain: bfloat16 [128], P('shard'), may hold values from 0.099609375 to 1.8984375
Outputs:
- output: bfloat16 [8192, 2048], P(('rep', 'shard'))
- input_grad: bfloat16 [8192, 2048], P(('rep', 'shard'))
- heads_grad: float32 [2048, 4096], P('shard')
- merge_grad: float32 [2048, 2048], P('shard')
- expand_grad: float32 [2048, 12288], P('shard')
- down_grad: float32 [6144, 2048], P('shard')
- first_grad: float32 [2048], P('shard')
- second_grad: float32 [2048], P('shard')
- query_grad: float32 [128], P('shard')
- key_grad: float32 [128], P('shard')
Inputs may be any that keep to these rules, and one draw needn't show every extreme that they name: `lengths`: row r belongs to device row r over rep+shard (rep the slower). An entry with length l > 0 and offset o holds one sequence in slots o to o + l - 1 of that device's 256 slots, with o + l <= 256; entries of a row never intersect; length 0 marks an empty entry. Some device holds one sequence of 256 tokens. `offsets`: first slot of each entry of lengths.
All inputs are finite; a program needn't handle non-finite values.
Results may differ from a plain program's by a relative error of at most 0.018.
Values may be sent and summed in bfloat16 or wider, within the bound.
No kernel may reach another device: no remote copies, remote signals or barrier semaphores. Data moves between devices by JAX's collectives and lax.ppermute only.
A program may use at most 448 MiB of HBM per device.

v0:
```python
import math
import jax
import jax.numpy as jnp
from jax import lax
from jax.sharding import PartitionSpec as P

QUERY_HEADS = 16
KEY_VALUE_HEADS = 8
HEAD_SIZE = 128
FF = 6144
EPS = 1e-06
THETA = 1000000.0
NEGATIVE = -1e30


def layout(lengths, offsets, slot_count):
    slots = jnp.arange(slot_count, dtype=jnp.int32)
    inside = (slots[:, None] >= offsets[None, :]) & (
        slots[:, None] < offsets[None, :] + lengths[None, :]
    )
    number = jnp.arange(lengths.shape[0], dtype=jnp.int32) + 1
    segment = jnp.sum(jnp.where(inside, number[None, :], 0), axis=1) - 1
    position = jnp.sum(jnp.where(inside, slots[:, None] - offsets[None, :], 0), axis=1)
    earlier = slots[None, :] <= slots[:, None]
    allowed = (segment[:, None] == segment[None, :]) & (segment[:, None] >= 0) & earlier
    allowed = allowed | (slots[None, :] == slots[:, None])
    expo = jnp.arange(HEAD_SIZE // 2, dtype=jnp.float32) * (2.0 / HEAD_SIZE)
    freq = jnp.power(THETA, -expo)
    angles = position.astype(jnp.float32)[:, None] * freq[None, :]
    return (allowed, jnp.cos(angles), jnp.sin(angles))


def apply_rotation(heads, cosine_table, sine_table):
    half = heads.shape[-1] // 2
    first = heads[..., :half]
    second = heads[..., half:]
    cosine_table = cosine_table[:, None, :]
    sine_table = sine_table[:, None, :]
    return jnp.concatenate(
        [first * cosine_table - second * sine_table, second * cosine_table + first * sine_table],
        axis=-1,
    )


def unrotate(grads, cosine_table, sine_table):
    half = grads.shape[-1] // 2
    first = grads[..., :half]
    second = grads[..., half:]
    cosine_table = cosine_table[:, None, :]
    sine_table = sine_table[:, None, :]
    return jnp.concatenate(
        [first * cosine_table + second * sine_table, second * cosine_table - first * sine_table],
        axis=-1,
    )


def norm_back(grads, unit, inverse, gain):
    scaled = grads * gain
    return inverse * (scaled - unit * jnp.mean(scaled * unit, axis=-1, keepdims=True))


def times_transposed(left, right):
    return lax.dot_general(
        left, right, (((1,), (1,)), ((), ())), preferred_element_type=jnp.float32
    )


def owner_rows(left, right):
    return lax.psum_scatter(
        lax.dot_general(
            left, right, (((0,), (0,)), ((), ())), preferred_element_type=jnp.float32
        ).astype(jnp.bfloat16),
        "shard",
        scatter_dimension=0,
        tiled=True,
    ).astype(jnp.float32)


def shards(
    hidden_in,
    cotangent,
    lengths,
    offsets,
    projection_weight,
    merge_weight,
    expand_weight,
    down_weight,
    first_gain,
    second_gain,
    query_norm_scale,
    key_gain,
):
    token_count = hidden_in.shape[0]
    head_group = QUERY_HEADS // KEY_VALUE_HEADS
    query_span = QUERY_HEADS * HEAD_SIZE
    key_span = KEY_VALUE_HEADS * HEAD_SIZE
    scale = 1.0 / math.sqrt(HEAD_SIZE)
    allowed, cosine_table, sine_table = layout(lengths[0], offsets[0], token_count)
    heads_full, merge_full, first_full, query_full, key_full = (
        lax.all_gather(projection_weight, "shard", axis=0, tiled=True),
        lax.all_gather(merge_weight, "shard", axis=0, tiled=True),
        lax.all_gather(first_gain, "shard", axis=0, tiled=True),
        lax.all_gather(query_norm_scale, "shard", axis=0, tiled=True),
        lax.all_gather(key_gain, "shard", axis=0, tiled=True),
    )
    first_scale = first_full.astype(jnp.float32)
    query_scale = query_full.astype(jnp.float32)
    key_scale = key_full.astype(jnp.float32)
    tokens = hidden_in.astype(jnp.float32)
    inverse_first = lax.rsqrt(jnp.mean(tokens * tokens, axis=1, keepdims=True) + EPS)
    unit_first = tokens * inverse_first
    normed = (unit_first * first_scale).astype(jnp.bfloat16)
    combined_projection = jnp.dot(normed, heads_full, preferred_element_type=jnp.float32)
    query_rows = combined_projection[:, :query_span].reshape(token_count, QUERY_HEADS, HEAD_SIZE)
    key_rows = combined_projection[:, query_span : query_span + key_span].reshape(
        token_count, KEY_VALUE_HEADS, HEAD_SIZE
    )
    value_rows = (
        combined_projection[:, query_span + key_span :]
        .reshape(token_count, KEY_VALUE_HEADS, HEAD_SIZE)
        .astype(jnp.bfloat16)
    )
    query_inverse = lax.rsqrt(jnp.mean(query_rows * query_rows, axis=-1, keepdims=True) + EPS)
    query_unit = query_rows * query_inverse
    key_inverse = lax.rsqrt(jnp.mean(key_rows * key_rows, axis=-1, keepdims=True) + EPS)
    key_unit = key_rows * key_inverse
    query_rotated = (
        apply_rotation(query_unit * query_scale, cosine_table, sine_table)
        .astype(jnp.bfloat16)
        .reshape(token_count, KEY_VALUE_HEADS, head_group, HEAD_SIZE)
    )
    key_rot = apply_rotation(key_unit * key_scale, cosine_table, sine_table).astype(jnp.bfloat16)
    scores = (
        jnp.einsum("qhgd,khd->hgqk", query_rotated, key_rot, preferred_element_type=jnp.float32)
        * scale
    )
    masked = jnp.where(allowed, scores, NEGATIVE)
    top = jnp.max(masked, axis=-1, keepdims=True)
    weights = jnp.where(allowed, jnp.exp(masked - top), 0.0)
    total = jnp.sum(weights, axis=-1, keepdims=True)
    logsum = top + jnp.log(total)
    probs = (weights / total).astype(jnp.bfloat16)
    context = jnp.einsum("hgqk,khd->qhgd", probs, value_rows, preferred_element_type=jnp.float32)
    context = context.reshape(token_count, query_span).astype(jnp.bfloat16)
    middle = tokens + jnp.dot(context, merge_full, preferred_element_type=jnp.float32)
    expand_full, down_full, second_full = (
        lax.all_gather(expand_weight, "shard", axis=0, tiled=True),
        lax.all_gather(down_weight, "shard", axis=0, tiled=True),
        lax.all_gather(second_gain, "shard", axis=0, tiled=True),
    )
    second_scale = second_full.astype(jnp.float32)
    inverse_second = lax.rsqrt(jnp.mean(middle * middle, axis=1, keepdims=True) + EPS)
    unit_second = middle * inverse_second
    normed_second = (unit_second * second_scale).astype(jnp.bfloat16)
    expanded = jnp.dot(normed_second, expand_full, preferred_element_type=jnp.float32)
    gates = expanded[:, :FF]
    ups = expanded[:, FF:]
    sigmoid = jax.nn.sigmoid(gates)
    activated = gates * sigmoid
    hidden = (activated * ups).astype(jnp.bfloat16)
    output = (middle + jnp.dot(hidden, down_full, preferred_element_type=jnp.float32)).astype(
        jnp.bfloat16
    )
    expand_back, down_back = (
        lax.all_gather(expand_weight, "shard", axis=0, tiled=True),
        lax.all_gather(down_weight, "shard", axis=0, tiled=True),
    )
    hidden_grad = times_transposed(cotangent, down_back)
    gate_grad = hidden_grad * ups * (sigmoid * (1.0 + gates * (1.0 - sigmoid)))
    up_grad = hidden_grad * activated
    expand_rows = jnp.concatenate([gate_grad, up_grad], axis=1).astype(jnp.bfloat16)
    second_back = times_transposed(expand_rows, expand_back)
    second_term = jnp.sum(second_back * unit_second, axis=0)
    middle_grad = cotangent.astype(jnp.float32) + norm_back(
        second_back, unit_second, inverse_second, second_scale
    )
    attention_rows = middle_grad.astype(jnp.bfloat16)
    heads_back, merge_back = (
        lax.all_gather(projection_weight, "shard", axis=0, tiled=True),
        lax.all_gather(merge_weight, "shard", axis=0, tiled=True),
    )
    context_grad = (
        times_transposed(attention_rows, merge_back)
        .astype(jnp.bfloat16)
        .reshape(token_count, KEY_VALUE_HEADS, head_group, HEAD_SIZE)
    )
    again_scores = (
        jnp.einsum("qhgd,khd->hgqk", query_rotated, key_rot, preferred_element_type=jnp.float32)
        * scale
    )
    probs_full = jnp.where(allowed, jnp.exp(again_scores - logsum), 0.0)
    probs_again = probs_full.astype(jnp.bfloat16)
    value_grad = jnp.einsum(
        "hgqk,qhgd->khd", probs_again, context_grad, preferred_element_type=jnp.float32
    )
    probs_grad = jnp.einsum(
        "qhgd,khd->hgqk", context_grad, value_rows, preferred_element_type=jnp.float32
    )
    delta = jnp.sum(probs_full * probs_grad, axis=-1, keepdims=True)
    score_grad = (probs_full * (probs_grad - delta)).astype(jnp.bfloat16)
    query_rot_grad = (
        jnp.einsum(
            "hgqk,khd->qhgd", score_grad, key_rot, preferred_element_type=jnp.float32
        ).reshape(token_count, QUERY_HEADS, HEAD_SIZE)
        * scale
    )
    key_rot_grad = (
        jnp.einsum("hgqk,qhgd->khd", score_grad, query_rotated, preferred_element_type=jnp.float32)
        * scale
    )
    query_normed_grad = unrotate(query_rot_grad, cosine_table, sine_table)
    key_normed_grad = unrotate(key_rot_grad, cosine_table, sine_table)
    query_term = jnp.sum(query_normed_grad * query_unit, axis=(0, 1))
    key_term = jnp.sum(key_normed_grad * key_unit, axis=(0, 1))
    query_back = norm_back(query_normed_grad, query_unit, query_inverse, query_scale)
    key_back = norm_back(key_normed_grad, key_unit, key_inverse, key_scale)
    united_rows = jnp.concatenate(
        [
            query_back.reshape(token_count, query_span),
            key_back.reshape(token_count, key_span),
            value_grad.reshape(token_count, key_span),
        ],
        axis=1,
    ).astype(jnp.bfloat16)
    first_back = times_transposed(united_rows, heads_back)
    first_term = jnp.sum(first_back * unit_first, axis=0)
    input_grad = (
        middle_grad + norm_back(first_back, unit_first, inverse_first, first_scale)
    ).astype(jnp.bfloat16)
    first_sum, second_sum, query_sum, key_sum = lax.psum(
        (first_term, second_term, query_term, key_term), ("rep", "shard")
    )
    index = lax.axis_index("shard")
    first_grad = lax.dynamic_slice_in_dim(
        first_sum, index * first_gain.shape[0], first_gain.shape[0]
    )
    second_grad = lax.dynamic_slice_in_dim(
        second_sum, index * second_gain.shape[0], second_gain.shape[0]
    )
    query_grad = lax.dynamic_slice_in_dim(
        query_sum, index * query_norm_scale.shape[0], query_norm_scale.shape[0]
    )
    key_grad = lax.dynamic_slice_in_dim(key_sum, index * key_gain.shape[0], key_gain.shape[0])
    heads_share = owner_rows(normed, united_rows)
    merge_share = owner_rows(context, attention_rows)
    expand_share = owner_rows(normed_second, expand_rows)
    down_share = owner_rows(hidden, cotangent)
    heads_grad, merge_grad, expand_grad, down_grad = (
        lax.psum(heads_share.astype(jnp.bfloat16), "rep").astype(jnp.float32),
        lax.psum(merge_share.astype(jnp.bfloat16), "rep").astype(jnp.float32),
        lax.psum(expand_share.astype(jnp.bfloat16), "rep").astype(jnp.float32),
        lax.psum(down_share.astype(jnp.bfloat16), "rep").astype(jnp.float32),
    )
    return (
        output,
        input_grad,
        heads_grad,
        merge_grad,
        expand_grad,
        down_grad,
        first_grad,
        second_grad,
        query_grad,
        key_grad,
    )


def solution(mesh):
    placed = (
        P(("rep", "shard"), None),
        P(("rep", "shard"), None),
        P(("rep", "shard"), None),
        P(("rep", "shard"), None),
        P("shard", None),
        P("shard", None),
        P("shard", None),
        P("shard", None),
        P("shard"),
        P("shard"),
        P("shard"),
        P("shard"),
    )
    return jax.shard_map(
        shards,
        mesh=mesh,
        in_specs=placed,
        out_specs=(
            P(("rep", "shard"), None),
            P(("rep", "shard"), None),
            P("shard", None),
            P("shard", None),
            P("shard", None),
            P("shard", None),
            P("shard"),
            P("shard"),
            P("shard"),
            P("shard"),
        ),
        check_vma=False,
    )
```

profile of v0, /device:TPU:0, one launch (start us, length us, event | category | flops | bytes accessed | tf_op | source)
XLA Modules:
  0.0 1668.1 jit_solution(12764290787771420811)
XLA Ops:
  10.1 10.4 all-gather
  22.4 14.2 all-reduce.4
  37.7 9.2 all-gather.1
  48.5 54.0 %all-gather.7.cloned.1.call-done = bf16[2048,4096]{1,0:T(8,128)(2,1)} async-done(((bf16[256,4096]{1,0:T(8,128)(2,1)}), bf16[2048,4096]{1,0:T(8,128)(2,1)}) %all-gather.7.cloned.1.call-update) | async-done | bytes 16777232 | tf_op jit(solution)/shard_map/all_gather | solution.py:100
  102.5 8.2 fusion.57
  128.8 29.9 %all-gather.9.cloned.1.call-done = bf16[2048,2048]{1,0:T(8,128)(2,1)} async-done(((bf16[256,2048]{1,0:T(8,128)(2,1)}), bf16[2048,2048]{1,0:T(8,128)(2,1)}) %all-gather.9.cloned.1.call-update) | async-done | bytes 8388624 | tf_op jit(solution)/shard_map/all_gather | solution.py:101
  158.7 7.4 multiply_reduce_fusion.3
  166.1 226.6 %all-gather.11.cloned.1.call-done = bf16[2048,12288]{1,0:T(8,128)(2,1)} async-done(((bf16[256,12288]{1,0:T(8,128)(2,1)}), bf16[2048,12288]{1,0:T(8,128)(2,1)}) %all-gather.11.cloned.1.call-update) | async-done | bytes 50331664 | tf_op jit(solution)/shard_map/all_gather | solution.py:147
  392.7 27.1 %fusion.75 = f32[256,12288]{1,0:T(8,128)} fusion(bf16[2048,12288]{1,0:T(8,128)(2,1)} %all-gather.11.cloned.1.call-done, f32[256,2048]{1,0:T(8,128)} %get-tuple-element.54, f32[2048]{0:T(1024)S(1)} %bitcast.201, f32[256]{0:T(256)S(1)} %add_rsqrt_fusion.2), kind=kOutput, calls=%fused_computation.152 | convolution fusion | flops 12886474752 | bytes 65020928 | tf_op jit(solution)/shard_map/dot_general | solution.py:155
  419.8 99.9 %all-gather.13.cloned.1.call-done = bf16[6144,2048]{1,0:T(8,128)(2,1)} async-done(((bf16[768,2048]{1,0:T(8,128)(2,1)}), bf16[6144,2048]{1,0:T(8,128)(2,1)}) %all-gather.13.cloned.1.call-update) | async-done | bytes 25165840 | tf_op jit(solution)/shard_map/all_gather | solution.py:148
  519.7 20.5 %multiply_convert_fusion.1 = (bf16[256,6144]{1,0:T(8,128)(2,1)}, bf16[256,6144]{1,0:T(8,128)(2,1)}, bf16[256,6144]{1,0:T(8,128)(2,1)}) fusion(f32[256,12288]{1,0:T(8,128)} %fusion.75, bf16[256,2048]{1,0:T(8,128)(2,1)} %param.13, bf16[6144,2048]{1,0:T(8,128)(2,1)} %all-gather.13.cloned.1.call-done), kind=kOutput, calls=%fused_computation.6 | convolution fusion | flops 6466043904 | bytes 48234496 | tf_op jit(solution)/shard_map/dot_general | solution.py:63
  540.2 24.4 %multiply_reduce_fusion = (f32[2048]{0:T(1024)}, f32[256]{0:T(256)S(1)}, f32[256,2048]{1,0:T(8,128)}) fusion(f32[256,2048]{1,0:T(8,128)} %get-tuple-element.54, f32[256]{0:T(256)S(1)} %add_rsqrt_fusion.2, f32[2048]{0:T(1024)S(1)} %bitcast.202, bf16[2048,12288]{1,0:T(8,128)(2,1)} %all-gather.11.cloned.1.call-done, bf16[256,6144]{1,0:T(8,128)(2,1)} %get-tuple-element.29, ...), kind=kOutput, calls=%fused_computation.54 | convolution fusion | flops 12900628480 | bytes 60835840 | tf_op jit(solution)/shard_map/dot_general | solution.py:63
  579.7 8.8 convolution_convert_fusion.4
  633.0 8.6 convolution_convert_fusion.2
  642.9 14.2 convolution_convert_fusion.1
  659.1 26.9 %convolution_convert_fusion = bf16[2048,12288]{1,0:T(8,128)(2,1)} fusion(bf16[256,6144]{1,0:T(8,128)(2,1)} %get-tuple-element.29, bf16[256,6144]{1,0:T(8,128)(2,1)} %get-tuple-element.28, f32[256,2048]{1,0:T(8,128)S(1)} %copy-done.3, f32[2048]{0:T(1024)S(1)} %bitcast.204, f32[256]{0:T(256)S(1)} %add_rsqrt_fusion.2), kind=kOutput, calls=%fused_computation | convolution fusion | flops 12924223488 | bytes 58729472 | tf_op jit(solution)/shard_map/dot_general | solution.py:70
  686.1 80.1 %reduce-scatter.7.cloned.1.call-done = bf16[256,4096]{1,0:T(8,128)(2,1)} async-done(((bf16[2048,4096]{1,0:T(8,128)(2,1)}), bf16[256,4096]{1,0:T(8,128)(2,1)}) %reduce-scatter.7.cloned.1.call-update) | async-done | bytes 2097168 | tf_op jit(solution)/shard_map/reduce_scatter | solution.py:69
  766.2 159.9 %reduce-scatter.11.cloned.1.call-done = bf16[768,2048]{1,0:T(8,128)(2,1)} async-done(((bf16[6144,2048]{1,0:T(8,128)(2,1)}), bf16[768,2048]{1,0:T(8,128)(2,1)}) %reduce-scatter.11.cloned.1.call-update) | async-done | bytes 3145744 | tf_op jit(solution)/shard_map/reduce_scatter | solution.py:69
  926.1 288.0 %reduce-scatter.13.cloned.1.call-done = bf16[256,12288]{1,0:T(8,128)(2,1)} async-done(((bf16[2048,12288]{1,0:T(8,128)(2,1)}), bf16[256,12288]{1,0:T(8,128)(2,1)}) %reduce-scatter.13.cloned.1.call-update) | async-done | bytes 6291472
  1214.2 12.6 fusion.23
  1226.8 45.0 %all-reduce.3 = (f32[2048]{0:T(1024)S(1)}, f32[2048]{0:T(1024)S(1)}, f32[128]{0:T(128)S(1)}, f32[128]{0:T(128)S(1)}) all-reduce(f32[2048]{0:T(1024)S(1)} %get-tuple-element.12, f32[2048]{0:T(1024)S(1)} %copy-done.41, f32[128]{0:T(128)S(1)} %bitcast_reduce_fusion, ...), channel_id=1, replica_groups=mesh['rep'=4,'shard'=8] {'rep','shard'}, use_global_device_ids=true, to_apply=%region_22.23 | all-reduce | flops 4352 | bytes 34816 | tf_op jit(solution)/shard_map/psum | solution.py:230
  1278.3 12.9 fusion.13
  1291.2 353.0 %all-reduce.8.cloned.1.call-done = (bf16[256,4096]{1,0:T(8,128)(2,1)}, bf16[256,2048]{1,0:T(8,128)(2,1)}, bf16[256,12288]{1,0:T(8,128)(2,1)}, bf16[768,2048]{1,0:T(8,128)(2,1)}) async-done(((bf16[256,4096]{1,0:T(8,128)(2,1)}, bf16[256,2048]{1,0:T(8,128)(2,1)}, bf16[256,12288]{1,0:T(8,128)(2,1)}, bf16[768,2048]{1,0:T(8,128)(2,1)}), (bf16[256,4096]{1,0:T(8,128)(2,1)}, bf16[256,2048]{1,0:T(8,128)(2,1)}, ...) | async-done | bytes 12582928 | tf_op jit(solution)/shard_map/psum | solution.py:249
  1644.2 9.2 convert_element_type.131
  (209 shorter events, 101.2 us)
Async XLA Ops:
  7.2 95.3 %all-gather.7.cloned.1.call-start = ((), (), s32[]{:S(2)}) async-start(), calls=%async_computation.4 | async-start | bytes 18874368 | tf_op jit(solution)/shard_map/all_gather | solution.py:100
  7.9 150.8 %all-gather.9.cloned.1.call-start = ((), (), s32[]{:S(2)}) async-start(), calls=%async_computation.5 | async-start | bytes 9437184 | tf_op jit(solution)/shard_map/all_gather | solution.py:101
  8.7 384.1 %all-gather.11.cloned.1.call-start = ((), (), s32[]{:S(2)}) async-start(), calls=%async_computation.6 | async-start | bytes 56623104 | tf_op jit(solution)/shard_map/all_gather | solution.py:147
  9.4 11.2 copy-start.52
  9.4 12.4 copy-start.48
  9.4 12.7 copy-start.49
  9.4 27.6 %copy-start.46 = (s32[1,4]{1,0:T(1,128)S(1)}, s32[1,4]{1,0:T(1,128)}, u32[]{:S(2)}) copy-start(s32[1,4]{1,0:T(1,128)} %param.15) | copy-start | bytes 52
  9.4 27.6 %copy-start.50 = (s32[1,4]{1,0:T(1,128)S(1)}, s32[1,4]{1,0:T(1,128)}, u32[]{:S(2)}) copy-start(s32[1,4]{1,0:T(1,128)} %param.14) | copy-start | bytes 52
  9.5 28.2 %copy-start.51 = (bf16[256]{0:T(256)(128)(2,1)S(1)}, bf16[256]{0:T(256)(128)(2,1)}, u32[]{:S(2)}) copy-start(bf16[256]{0:T(256)(128)(2,1)} %param.21) | copy-start | bytes 1540
  9.5 37.4 %copy-start.2 = (bf16[256,2048]{1,0:T(8,128)(2,1)S(1)}, bf16[256,2048]{1,0:T(8,128)(2,1)}, u32[]{:S(2)}) copy-start(bf16[256,2048]{1,0:T(8,128)(2,1)} %param.12) | copy-start | bytes 3145732
  9.5 510.2 %all-gather.13.cloned.1.call-start = ((), (), s32[]{:S(2)}) async-start(), calls=%async_computation.7 | async-start | bytes 28311552 | tf_op jit(solution)/shard_map/all_gather | solution.py:148
  10.1 676.0 %reduce-scatter.9.cloned.1.call-start = ((), (), s32[]{:S(2)}) async-start(), calls=%async_computation.9 | async-start | bytes 9437184 | tf_op jit(solution)/shard_map/reduce_scatter | solution.py:69
  20.6 90.1 %copy-start.31 = (f32[8,1,256]{2,1,0:T(1,128)}, f32[8,1,256]{2,1,0:T(1,128)S(1)}, u32[]{:S(2)}) copy-start(f32[8,1,256]{2,1,0:T(1,128)S(1)} %convert_element_type.134) | copy-start | bytes 24580
  47.2 63.5 %copy-start.39 = (f32[256]{0:T(256)}, f32[256]{0:T(256)S(1)}, u32[]{:S(2)}) copy-start(f32[256]{0:T(256)S(1)} %add_rsqrt_fusion.3) | copy-start | bytes 3076
  121.0 4.4 copy-start.25
  564.6 4.5 copy-start.12
  574.9 191.3 %reduce-scatter.7.cloned.1.call-start = ((), (), s32[]{:S(2)}) async-start(), calls=%async_computation.8 | async-start | bytes 18874368 | tf_op jit(solution)/shard_map/reduce_scatter | solution.py:69
  628.4 4.6 copy-start.23
  632.9 8.7 copy-start.19
  641.7 284.5 %reduce-scatter.11.cloned.1.call-start = ((), (), s32[]{:S(2)}) async-start(), calls=%async_computation.10 | async-start | bytes 28311552 | tf_op jit(solution)/shard_map/reduce_scatter | solution.py:69
  657.0 557.1 %reduce-scatter.13.cloned.1.call-start = ((), (), s32[]{:S(2)}) async-start(), calls=%async_computation.11 | async-start | bytes 56623104
  686.0 958.2 %all-reduce.8.cloned.1.call-start = ((), (), s32[]{:S(2)}) async-start(), calls=%async_computation.12 | async-start | bytes 25165824 | tf_op jit(solution)/shard_map/psum | solution.py:249
  1214.2 12.6 copy-start.41
  1644.2 9.2 copy-start.21
  (38 other events, 86.1 us)
Sparse Core Ops, SparseCore 0:
  9.9 92.6 all-gather.6
  104.4 54.2 all-gather.8
  160.6 232.0 all-gather.10
  394.5 125.1 all-gather.12
  575.0 71.4 reduce-scatter.8
  650.0 116.1 reduce-scatter.6
  769.8 156.2 reduce-scatter.10
  929.8 284.3 reduce-scatter.12
  1217.0 427.1 all-reduce.7
where the time goes:
time: 1670 us
  waiting for transfers between devices  1290 us (77%)
  matrix products  194 us (12%)
  blocking collectives  78.8 us (5%)
  other arithmetic  45.5 us (3%)
  local copies, waits for them, and re-layouts  39.6 us (2%)
    psum x1, waiting for transfers between devices, shards(): lax.psum(heads_share.astype(jnp.bfloat16), 'rep').astype(jnp.float32)  353 us
    unnamed x10, waiting for transfers between devices  291 us
    reduce_scatter x3, waiting for transfers between devices, owner_rows(): lax.psum_scatter(lax.dot_general(left, right, (((0,), (0,)), ((), ())), p...  240 us
    all_gather x1, waiting for transfers between devices, shards(): lax.all_gather(expand_weight, 'shard', axis=0, tiled=True)  227 us
    all_gather x1, waiting for transfers between devices, shards(): lax.all_gather(down_weight, 'shard', axis=0, tiled=True)  99.9 us
    dot_general x4, matrix products, times_transposed(): lax.dot_general(left, right, (((1,), (1,)), ((), ())), preferred_element_...  66.3 us
    dot_general x4, matrix products, owner_rows(): lax.dot_general(left, right, (((0,), (0,)), ((), ())), preferred_element_...  55.5 us
    all_gather x1, waiting for transfers between devices, shards(): lax.all_gather(projection_weight, 'shard', axis=0, tiled=True)  54 us
  transfers between devices with their start and end apart: 9, of which 8 were waited for; matrix products, arithmetic and copies ran while one was open for 12% of the time, Pallas kernels for 0%

commit v1 on v0

--- a/solution.py
+++ b/solution.py
@@ -11,6 +11,12 @@
 EPS = 1e-06
 THETA = 1000000.0
 NEGATIVE = -1e30
+
+
+def add_all(x, axis):
+    parts = lax.all_gather(x, axis, axis=0, tiled=False)
+    total = parts.sum(axis=0)
+    return total
 
 
 def layout(lengths, offsets, slot_count):
@@ -246,7 +252,7 @@
     expand_share = owner_rows(normed_second, expand_rows)
     down_share = owner_rows(hidden, cotangent)
     heads_grad, merge_grad, expand_grad, down_grad = (
-        lax.psum(heads_share.astype(jnp.bfloat16), "rep").astype(jnp.float32),
+        add_all(heads_share.astype(jnp.bfloat16), "rep").astype(jnp.float32),
         lax.psum(merge_share.astype(jnp.bfloat16), "rep").astype(jnp.float32),
         lax.psum(expand_share.astype(jnp.bfloat16), "rep").astype(jnp.float32),
         lax.psum(down_share.astype(jnp.bfloat16), "rep").astype(jnp.float32),

time: 1670 us -> 1810 us (1.084)
  waiting for transfers between devices: 1290 us -> 1420 us
    all_gather x0 -> x1, waiting for transfers between devices: none -> 72.2 us  [add_all(): parts = lax.all_gather(x, axis, axis=0, tiled=False)]
    reduce_scatter x3, waiting for transfers between devices: 240 us -> 298 us  [owner_rows(): lax.psum_scatter(lax.dot_general(left, right, (((0,), (0,)), ((), ())), p...]
    unnamed x10 -> x11, waiting for transfers between devices: 291 us -> 291 us
  transfers between devices with their start and end apart: 9 -> 10, of which waited for: 8 -> 10; matrix products, arithmetic and copies ran while one was open for 12% -> 9% of each run, Pallas kernels for 0% -> 0%
where the time goes in v1:
time: 1810 us; the launch traced here: 1800 us
  waiting for transfers between devices  1420 us (78%)
  matrix products  190 us (10%)
  blocking collectives  81.9 us (5%)
  other arithmetic  52.4 us (3%)
  local copies, waits for them, and re-layouts  41.7 us (2%)
    psum x1, waiting for transfers between devices, shards(): lax.psum(merge_share.astype(jnp.bfloat16), 'rep').astype(jnp.float32)  352 us
    reduce_scatter x3, waiting for transfers between devices, owner_rows(): lax.psum_scatter(lax.dot_general(left, right, (((0,), (0,)), ((), ())), p...  298 us
    unnamed x11, waiting for transfers between devices  291 us
    all_gather x1, waiting for transfers between devices, shards(): lax.all_gather(expand_weight, 'shard', axis=0, tiled=True)  226 us
    all_gather x1, waiting for transfers between devices, shards(): lax.all_gather(down_weight, 'shard', axis=0, tiled=True)  99.8 us
    all_gather x1, waiting for transfers between devices, add_all(): parts = lax.all_gather(x, axis, axis=0, tiled=False)  72.2 us
    dot_general x4, matrix products, times_transposed(): lax.dot_general(left, right, (((1,), (1,)), ((), ())), preferred_element_...  64.1 us
    dot_general x4, matrix products, owner_rows(): lax.dot_general(left, right, (((0,), (0,)), ((), ())), preferred_element_...  57.7 us
  transfers between devices with their start and end apart: 10, of which 10 were waited for; matrix products, arithmetic and copies ran while one was open for 9% of the time, Pallas kernels for 0%

profile of v1, /device:TPU:0, one launch (start us, length us, event | category | flops | bytes accessed | tf_op | source)
XLA Modules:
  0.0 1799.4 jit_solution(1155087046700060400)
XLA Ops:
  10.1 10.4 all-gather.1
  22.4 14.2 all-reduce.4
  36.7 9.2 all-gather.2
  48.7 53.9 %all-gather.9.cloned.1.call-done = bf16[2048,4096]{1,0:T(8,128)(2,1)} async-done(((bf16[256,4096]{1,0:T(8,128)(2,1)}), bf16[2048,4096]{1,0:T(8,128)(2,1)}) %all-gather.9.cloned.1.call-update) | async-done | bytes 16777232 | tf_op jit(solution)/shard_map/all_gather | solution.py:106
  102.6 8.2 fusion.57
  133.6 25.2 %all-gather.11.cloned.1.call-done = bf16[2048,2048]{1,0:T(8,128)(2,1)} async-done(((bf16[256,2048]{1,0:T(8,128)(2,1)}), bf16[2048,2048]{1,0:T(8,128)(2,1)}) %all-gather.11.cloned.1.call-update) | async-done | bytes 8388624 | tf_op jit(solution)/shard_map/all_gather | solution.py:107
  166.9 226.0 %all-gather.13.cloned.1.call-done = bf16[2048,12288]{1,0:T(8,128)(2,1)} async-done(((bf16[256,12288]{1,0:T(8,128)(2,1)}), bf16[2048,12288]{1,0:T(8,128)(2,1)}) %all-gather.13.cloned.1.call-update) | async-done | bytes 50331664 | tf_op jit(solution)/shard_map/all_gather | solution.py:153
  392.8 27.1 %fusion.75 = f32[256,12288]{1,0:T(8,128)} fusion(bf16[2048,12288]{1,0:T(8,128)(2,1)} %all-gather.13.cloned.1.call-done, f32[256,2048]{1,0:T(8,128)} %get-tuple-element.53, f32[2048]{0:T(1024)S(1)} %bitcast.203, f32[256]{0:T(256)S(1)} %add_rsqrt_fusion.2), kind=kOutput, calls=%fused_computation.152 | convolution fusion | flops 12886474752 | bytes 65020928 | tf_op jit(solution)/shard_map/dot_general | solution.py:161
  420.0 99.8 %all-gather.15.cloned.1.call-done = bf16[6144,2048]{1,0:T(8,128)(2,1)} async-done(((bf16[768,2048]{1,0:T(8,128)(2,1)}), bf16[6144,2048]{1,0:T(8,128)(2,1)}) %all-gather.15.cloned.1.call-update) | async-done | bytes 25165840 | tf_op jit(solution)/shard_map/all_gather | solution.py:154
  519.8 20.4 %multiply_convert_fusion.1 = (bf16[256,6144]{1,0:T(8,128)(2,1)}, bf16[256,6144]{1,0:T(8,128)(2,1)}, bf16[256,6144]{1,0:T(8,128)(2,1)}) fusion(f32[256,12288]{1,0:T(8,128)} %fusion.75, bf16[256,2048]{1,0:T(8,128)(2,1)} %param.13, bf16[6144,2048]{1,0:T(8,128)(2,1)} %all-gather.15.cloned.1.call-done), kind=kOutput, calls=%fused_computation.6 | convolution fusion | flops 6466043904 | bytes 48234496 | tf_op jit(solution)/shard_map/dot_general | solution.py:69
  540.2 24.5 %multiply_reduce_fusion = (f32[2048]{0:T(1024)}, f32[256]{0:T(256)S(1)}, f32[256,2048]{1,0:T(8,128)}) fusion(f32[256,2048]{1,0:T(8,128)} %get-tuple-element.53, f32[256]{0:T(256)S(1)} %add_rsqrt_fusion.2, f32[2048]{0:T(1024)S(1)} %bitcast.204, bf16[2048,12288]{1,0:T(8,128)(2,1)} %all-gather.13.cloned.1.call-done, bf16[256,6144]{1,0:T(8,128)(2,1)} %get-tuple-element.28, ...), kind=kOutput, calls=%fused_computation.54 | convolution fusion | flops 12900628480 | bytes 60835840 | tf_op jit(solution)/shard_map/dot_general | solution.py:69
  617.8 8.6 convolution_convert_fusion.2
  636.8 18.2 %convolution_convert_fusion.1 = bf16[6144,2048]{1,0:T(8,128)(2,1)} fusion(bf16[256,6144]{1,0:T(8,128)(2,1)} %get-tuple-element.29, bf16[256,2048]{1,0:T(8,128)(2,1)S(1)} %copy-done.20), kind=kOutput, calls=%fused_computation.1 | convolution fusion | flops 6455033856 | bytes 29360128 | tf_op jit(solution)/shard_map/dot_general | solution.py:76
  656.6 23.7 %convolution_convert_fusion = bf16[2048,12288]{1,0:T(8,128)(2,1)} fusion(bf16[256,6144]{1,0:T(8,128)(2,1)} %get-tuple-element.28, bf16[256,6144]{1,0:T(8,128)(2,1)} %get-tuple-element.27, f32[256,2048]{1,0:T(8,128)S(1)} %copy-done.3, f32[2048]{0:T(1024)S(1)} %bitcast.206, f32[256]{0:T(256)S(1)} %add_rsqrt_fusion.2), kind=kOutput, calls=%fused_computation | convolution fusion | flops 12924223488 | bytes 58729472 | tf_op jit(solution)/shard_map/dot_general | solution.py:76
  680.3 62.5 %reduce-scatter.7.cloned.1.call-done = bf16[256,4096]{1,0:T(8,128)(2,1)} async-done(((bf16[2048,4096]{1,0:T(8,128)(2,1)}), bf16[256,4096]{1,0:T(8,128)(2,1)}) %reduce-scatter.7.cloned.1.call-update) | async-done | bytes 2097168 | tf_op jit(solution)/shard_map/reduce_scatter | solution.py:75
  742.8 75.4 %reduce-scatter.9.cloned.1.call-done = bf16[256,2048]{1,0:T(8,128)(2,1)} async-done(((bf16[2048,2048]{1,0:T(8,128)(2,1)}), bf16[256,2048]{1,0:T(8,128)(2,1)}) %reduce-scatter.9.cloned.1.call-update) | async-done | bytes 1048592 | tf_op jit(solution)/shard_map/reduce_scatter | solution.py:75
  818.2 159.9 %reduce-scatter.11.cloned.1.call-done = bf16[768,2048]{1,0:T(8,128)(2,1)} async-done(((bf16[6144,2048]{1,0:T(8,128)(2,1)}), bf16[768,2048]{1,0:T(8,128)(2,1)}) %reduce-scatter.11.cloned.1.call-update) | async-done | bytes 3145744 | tf_op jit(solution)/shard_map/reduce_scatter | solution.py:75
  978.2 288.0 %reduce-scatter.13.cloned.1.call-done = bf16[256,12288]{1,0:T(8,128)(2,1)} async-done(((bf16[2048,12288]{1,0:T(8,128)(2,1)}), bf16[256,12288]{1,0:T(8,128)(2,1)}) %reduce-scatter.13.cloned.1.call-update) | async-done | bytes 6291472
  1266.2 12.6 fusion.23
  1278.8 48.1 %all-reduce.3 = (f32[2048]{0:T(1024)S(1)}, f32[2048]{0:T(1024)S(1)}, f32[128]{0:T(128)S(1)}, f32[128]{0:T(128)S(1)}) all-reduce(f32[2048]{0:T(1024)S(1)} %get-tuple-element.12, f32[2048]{0:T(1024)S(1)} %copy-done.47, f32[128]{0:T(128)S(1)} %bitcast_reduce_fusion, ...), channel_id=1, replica_groups=mesh['rep'=4,'shard'=8] {'rep','shard'}, use_global_device_ids=true, to_apply=%region_22.23 | all-reduce | flops 4352 | bytes 34816 | tf_op jit(solution)/shard_map/psum | solution.py:236
  1333.3 12.9 fusion.13
  1346.2 72.2 %all-gather.17.cloned.1.call-done = bf16[1024,4096]{1,0:T(8,128)(2,1)} async-done(((bf16[256,4096]{1,0:T(8,128)(2,1)}), bf16[1024,4096]{1,0:T(8,128)(2,1)}) %all-gather.17.cloned.1.call-update) | async-done | bytes 8388624 | tf_op jit(solution)/shard_map/all_gather | solution.py:17
  1426.3 351.6 %all-reduce.8.cloned.1.call-done = (bf16[256,2048]{1,0:T(8,128)(2,1)}, bf16[256,12288]{1,0:T(8,128)(2,1)}, bf16[768,2048]{1,0:T(8,128)(2,1)}) async-done(((bf16[256,2048]{1,0:T(8,128)(2,1)}, bf16[256,12288]{1,0:T(8,128)(2,1)}, bf16[768,2048]{1,0:T(8,128)(2,1)}), (bf16[256,2048]{1,0:T(8,128)(2,1)}, bf16[256,12288]{1,0:T(8,128)(2,1)}, bf16[768,2048]{1,0:T(8,128)(2,1)})) %all-reduce.8.cloned.1.call-update) | async-done | bytes 10485776 | tf_op jit(solution)/shard_map/psum | solution.py:256
  1777.8 9.2 convert_element_type.133
  (225 shorter events, 121.8 us)
Async XLA Ops:
  7.2 95.4 %all-gather.9.cloned.1.call-start = ((), (), s32[]{:S(2)}) async-start(), calls=%async_computation.4 | async-start | bytes 18874368 | tf_op jit(solution)/shard_map/all_gather | solution.py:106
  7.9 150.9 %all-gather.11.cloned.1.call-start = ((), (), s32[]{:S(2)}) async-start(), calls=%async_computation.5 | async-start | bytes 9437184 | tf_op jit(solution)/shard_map/all_gather | solution.py:107
  8.7 384.2 %all-gather.13.cloned.1.call-start = ((), (), s32[]{:S(2)}) async-start(), calls=%async_computation.6 | async-start | bytes 56623104 | tf_op jit(solution)/shard_map/all_gather | solution.py:153
  9.4 11.2 copy-start.58
  9.4 12.4 copy-start.54
  9.4 12.7 copy-start.55
  9.4 27.1 %copy-start.52 = (s32[1,4]{1,0:T(1,128)S(1)}, s32[1,4]{1,0:T(1,128)}, u32[]{:S(2)}) copy-start(s32[1,4]{1,0:T(1,128)} %param.15) | copy-start | bytes 52
  9.4 27.1 %copy-start.56 = (s32[1,4]{1,0:T(1,128)S(1)}, s32[1,4]{1,0:T(1,128)}, u32[]{:S(2)}) copy-start(s32[1,4]{1,0:T(1,128)} %param.14) | copy-start | bytes 52
  9.5 27.2 %copy-start.57 = (bf16[256]{0:T(256)(128)(2,1)S(1)}, bf16[256]{0:T(256)(128)(2,1)}, u32[]{:S(2)}) copy-start(bf16[256]{0:T(256)(128)(2,1)} %param.21) | copy-start | bytes 1540
  9.5 36.5 %copy-start.2 = (bf16[256,2048]{1,0:T(8,128)(2,1)S(1)}, bf16[256,2048]{1,0:T(8,128)(2,1)}, u32[]{:S(2)}) copy-start(bf16[256,2048]{1,0:T(8,128)(2,1)} %param.12) | copy-start | bytes 3145732
  9.5 510.3 %all-gather.15.cloned.1.call-start = ((), (), s32[]{:S(2)}) async-start(), calls=%async_computation.7 | async-start | bytes 28311552 | tf_op jit(solution)/shard_map/all_gather | solution.py:154
  10.1 732.7 %reduce-scatter.7.cloned.1.call-start = ((), (), s32[]{:S(2)}) async-start(), calls=%async_computation.8 | async-start | bytes 18874368 | tf_op jit(solution)/shard_map/reduce_scatter | solution.py:75
  20.6 90.2 %copy-start.33 = (f32[8,1,256]{2,1,0:T(1,128)}, f32[8,1,256]{2,1,0:T(1,128)S(1)}, u32[]{:S(2)}) copy-start(f32[8,1,256]{2,1,0:T(1,128)S(1)} %convert_element_type.136) | copy-start | bytes 24580
  36.5 74.3 %copy-start.48 = (f32[128]{0:T(128)}, f32[128]{0:T(128)S(1)}, u32[]{:S(2)}) copy-start(f32[128]{0:T(128)S(1)} %convert_element_type.111) | copy-start | bytes 1540
  36.7 81.4 %copy-start.50 = (f32[128]{0:T(128)}, f32[128]{0:T(128)S(1)}, u32[]{:S(2)}) copy-start(f32[128]{0:T(128)S(1)} %convert_element_type.113) | copy-start | bytes 1540
  46.3 64.5 %copy-start.44 = (f32[256]{0:T(256)}, f32[256]{0:T(256)S(1)}, u32[]{:S(2)}) copy-start(f32[256]{0:T(256)S(1)} %add_rsqrt_fusion.3) | copy-start | bytes 3076
  617.6 8.9 copy-start.25
  626.5 191.7 %reduce-scatter.9.cloned.1.call-start = ((), (), s32[]{:S(2)}) async-start(), calls=%async_computation.9 | async-start | bytes 9437184 | tf_op jit(solution)/shard_map/reduce_scatter | solution.py:75
  635.3 342.8 %reduce-scatter.11.cloned.1.call-start = ((), (), s32[]{:S(2)}) async-start(), calls=%async_computation.10 | async-start | bytes 28311552 | tf_op jit(solution)/shard_map/reduce_scatter | solution.py:75
  655.0 611.1 %reduce-scatter.13.cloned.1.call-start = ((), (), s32[]{:S(2)}) async-start(), calls=%async_computation.12 | async-start | bytes 56623104
  680.3 738.1 %all-gather.17.cloned.1.call-start = ((), (), s32[]{:S(2)}) async-start(), calls=%async_computation.11 | async-start | bytes 10485760 | tf_op jit(solution)/shard_map/all_gather | solution.py:17
  742.8 1035.0 %all-reduce.8.cloned.1.call-start = ((), (), s32[]{:S(2)}) async-start(), calls=%async_computation.13 | async-start | bytes 20971520 | tf_op jit(solution)/shard_map/psum | solution.py:256
  1266.2 12.6 copy-start.47
  1777.8 9.2 copy-start.24
  (45 other events, 121.4 us)
Sparse Core Ops, SparseCore 0:
  9.9 92.6 all-gather.8
  104.5 54.2 all-gather.10
  160.7 232.0 all-gather.12
  394.6 125.1 all-gather.14
  626.6 116.1 reduce-scatter.6
  746.7 71.5 reduce-scatter.8
  821.8 156.2 reduce-scatter.10
  981.8 284.3 reduce-scatter.12
  1267.7 150.6 all-gather.16
  1421.1 356.7 all-reduce.7
